TPU v7x, 32 devices: a whole 2x2x4 slice. The times are simulated.
32 devices in a mesh: groups: 2 (over y), dp: 4 (over z), tgt: 4 (over x, core).
Axes of the slice: x: 2, y: 2, z: 4, core: 2. Of those that a mesh axis runs over, the one named last changes fastest.
Arguments:
- hidden: bfloat16 [6144, 4096], P(('groups', 'dp', 'tgt')), parts along dimension 0, may hold values from -6 to 6
- cotangent: bfloat16 [6144, 4096], P(('groups', 'dp', 'tgt')), parts along dimension 0, may hold values from -6 to 6
- adapter_down_weight: bfloat16 [4096, 64], replicated, may hold values from -0.09375 to 0.09375
- adapter_up_weight: bfloat16 [64, 4096], replicated, may hold values from -0.75 to 0.75
- width_projection_factor: bfloat16 [4096, 512], replicated, may hold values from -0.09375 to 0.09375
- rank_projection_factor: bfloat16 [64, 8], replicated, may hold values from -0.75 to 0.75
- targets: bfloat16 [8, 768, 8192], P(('groups', 'dp'), 'tgt'), parts along dimension 0, may hold values from -100 to 100
- strata: int32 [768], P(('groups', 'dp', 'tgt')), parts along dimension 0, may hold values from 0 to 31
- keep: int32 [768], P(('groups', 'dp', 'tgt')), parts along dimension 0, may hold values from 0 to 1
- shard_example_count: int32 [32], P(('groups', 'dp', 'tgt')), parts along dimension 0, may hold values from 18 to 24
- stratum_owner_table: int32 [32], replicated, may hold values from 0 to 3, as said below
Outputs:
- selection: float32 [768], P(('groups', 'dp', 'tgt')), parts along dimension 0
There are 2 independent parts, one for each index of `groups`. A program takes and returns all parts, laid end to end along the dimension named above; an argument that names none is the same for every part. Nothing has to cross between parts.
Inputs may be any that keep to these rules, and one draw needn't show every extreme that they name: `stratum_owner_table`: each of the 4 owners holds exactly 8 strata.
All inputs are finite; a program needn't handle non-finite values.
Results may differ from a plain program's by a relative error of at most 0.0029.
Values may be sent and summed in bfloat16 or wider, within the bound.
A program may use at most 64 MiB of HBM per device.

v0:
```python
import math
import jax
import jax.numpy as jnp
from jax import lax
from jax.sharding import PartitionSpec as P

FEAT = 8192
CAP = 2
TGT = 768
TASKS = 16
epsilon = 1e-06


def contracted_row_sums(row_block, col_block):
    return lax.dot_general(
        row_block, col_block, (((1,), (1,)), ((), ())), preferred_element_type=jnp.float32
    )


def inverse_norms(values):
    widened = values.astype(jnp.float32)
    return lax.rsqrt(jnp.sum(widened * widened, axis=1) + epsilon)


def task_terms(row_block, row_inv, col_block, col_inv, first_index):
    per_task = TGT // TASKS
    products = contracted_row_sums(row_block, col_block)
    aligned = math.sqrt(FEAT) * products * row_inv[:, None] * col_inv[None, :]
    target_ids = (first_index + jnp.arange(col_block.shape[0], dtype=jnp.int32)) // per_task
    task_mask = (target_ids[:, None] == jnp.arange(TASKS, dtype=jnp.int32)[None, :]).astype(
        jnp.float32
    )
    return jnp.dot(jnp.maximum(aligned, 0.0), task_mask, precision=lax.Precision.HIGHEST)


def per_example(values, examples):
    return values.reshape(examples, -1, values.shape[1])


def shards(
    hidden,
    cotangent,
    adapter_down_weight,
    adapter_up_weight,
    width_projection_factor,
    rank_projection_factor,
    targets,
    strata,
    keep,
    shard_example_count,
    stratum_owner_table,
):
    examples = strata.shape[0]
    strata_total = stratum_owner_table.shape[0]
    ordinal = jnp.arange(examples, dtype=jnp.int32)
    usable = ordinal < shard_example_count[0]
    is_live = jnp.logical_and(keep == 1, usable)
    member = strata[:, None] == jnp.arange(strata_total, dtype=jnp.int32)[None, :]
    local_counts = jnp.sum(jnp.logical_and(member, is_live[:, None]).astype(jnp.float32), axis=0)
    counts = lax.psum(local_counts, ("dp", "tgt"))
    down_activation = jnp.dot(
        hidden, adapter_down_weight, preferred_element_type=jnp.float32
    ).astype(jnp.bfloat16)
    up_backward_product = contracted_row_sums(cotangent, adapter_up_weight).astype(jnp.bfloat16)
    wide_hidden = jnp.dot(
        hidden, width_projection_factor, preferred_element_type=jnp.float32
    ).astype(jnp.bfloat16)
    wide_back = jnp.dot(
        cotangent, width_projection_factor, preferred_element_type=jnp.float32
    ).astype(jnp.bfloat16)
    rank_down = jnp.dot(
        down_activation, rank_projection_factor, preferred_element_type=jnp.float32
    ).astype(jnp.bfloat16)
    rank_up = jnp.dot(
        up_backward_product, rank_projection_factor, preferred_element_type=jnp.float32
    ).astype(jnp.bfloat16)
    up_grad = jnp.einsum(
        "esr,esd->erd",
        per_example(rank_down, examples),
        per_example(wide_back, examples),
        preferred_element_type=jnp.float32,
    )
    down_grad = jnp.einsum(
        "esd,esr->edr",
        per_example(wide_hidden, examples),
        per_example(rank_up, examples),
        preferred_element_type=jnp.float32,
    )
    features = jnp.concatenate(
        [up_grad.reshape(examples, -1), down_grad.reshape(examples, -1)], axis=1
    ).astype(jnp.bfloat16)
    owner_of = jnp.sum(jnp.where(member, stratum_owner_table[None, :], 0), axis=1)
    earlier = ordinal[:, None] > ordinal[None, :]
    same_owner = owner_of[:, None] == owner_of[None, :]
    ahead = jnp.logical_and(jnp.logical_and(earlier, same_owner), is_live[None, :])
    slot_rank = jnp.sum(ahead.astype(jnp.int32), axis=1)
    is_sent = jnp.logical_and(is_live, slot_rank < CAP)
    owner_count = lax.axis_size("dp")
    slot_index = owner_of * CAP + slot_rank
    slot_ids = jnp.arange(owner_count * CAP, dtype=jnp.int32)
    dispatch = jnp.logical_and(slot_ids[:, None] == slot_index[None, :], is_sent[None, :])
    outgoing = jnp.dot(
        dispatch.astype(jnp.bfloat16), features, preferred_element_type=jnp.float32
    ).astype(jnp.bfloat16)
    received = lax.all_to_all(
        outgoing.reshape(owner_count, CAP, -1), "dp", split_axis=0, concat_axis=0, tiled=True
    )
    owner_rows = received.reshape(owner_count * CAP, -1)
    own_targets = targets[0]
    target_inv = inverse_norms(own_targets)
    offset = lax.axis_index("tgt") * own_targets.shape[0]
    row_piece = lax.all_gather(owner_rows, "tgt", axis=0, tiled=True)
    partials = task_terms(row_piece, inverse_norms(row_piece), own_targets, target_inv, offset)
    task_sums = lax.psum_scatter(partials, "tgt", scatter_dimension=0, tiled=True)
    raw_owner = jnp.max(task_sums / (TGT // TASKS), axis=1)
    returned = lax.all_to_all(
        raw_owner.reshape(owner_count, CAP), "dp", split_axis=0, concat_axis=0, tiled=True
    ).reshape(owner_count * CAP)
    raw_score = jnp.sum(jnp.where(dispatch, returned[:, None], 0.0), axis=0)
    stratum_count = jnp.sum(jnp.where(member, counts[None, :], 0.0), axis=1)
    weight = jnp.sqrt(jnp.sum(counts) / (strata_total * jnp.maximum(stratum_count, 1.0)))
    return jnp.where(is_sent, raw_score * weight, 0.0)


def solution(mesh):
    return jax.shard_map(
        shards,
        mesh=mesh,
        in_specs=(
            P(("groups", "dp", "tgt"), None),
            P(("groups", "dp", "tgt"), None),
            P(),
            P(),
            P(),
            P(),
            P(("groups", "dp"), "tgt", None),
            P(("groups", "dp", "tgt")),
            P(("groups", "dp", "tgt")),
            P(("groups", "dp", "tgt")),
            P(),
        ),
        out_specs=P(("groups", "dp", "tgt")),
        check_vma=False,
    )
```

profile of v0, /device:TPU:0, one launch (start us, length us, event | category | flops | bytes accessed | tf_op | source)
XLA Modules:
  0.0 93.7 jit_solution(1229232755631329175)
XLA Ops:
  0.8 0.7 compare_and_fusion.1
  1.4 0.9 select_reduce_fusion.1
  2.3 0.2 convert_reduce_fusion.1
  2.5 0.7 compare_and_fusion
  3.2 2.3 %fusion.15 = bf16[192,8]{0,1:T(8,128)(2,1)S(1)} fusion(bf16[64,8]{0,1:T(8,128)(2,1)} %param.16, bf16[192,4096]{1,0:T(8,128)(2,1)} %param.12, bf16[64,4096]{1,0:T(8,128)(2,1)} %param.14), kind=kOutput, calls=%fused_computation.17 | convolution fusion | flops 100873728 | bytes 2101248 | tf_op jit(solution)/shard_map/dot_general | solution.py:74
  5.5 0.1 reshape.70
  5.6 3.3 %convolution_convert_fusion.1 = bf16[24,512,8]{1,2,0:T(8,128)(2,1)S(1)} fusion(bf16[192,4096]{1,0:T(8,128)(2,1)S(1)} %copy-done, bf16[4096,512]{1,0:T(8,128)(2,1)} %param.15, bf16[24,8,8]{1,0,2:T(8,128)(2,1)S(1)} %reshape.70), kind=kOutput, calls=%fused_computation.4 | convolution fusion | flops 807075840 | bytes 5966848 | tf_op jit(solution)/shard_map/esd,esr->edr/dot_general | solution.py:83
  8.9 0.8 copy.25
  9.8 0.3 copy.26
  10.1 1.9 %fusion.16 = bf16[192,8]{0,1:T(8,128)(2,1)S(1)} fusion(bf16[64,8]{0,1:T(8,128)(2,1)S(1)} %copy-done.2, bf16[192,4096]{1,0:T(8,128)(2,1)S(1)} %copy-done, bf16[4096,64]{0,1:T(8,128)(2,1)} %param.13), kind=kOutput, calls=%fused_computation.18 | convolution fusion | flops 100873728 | bytes 2101248 | tf_op jit(solution)/shard_map/dot_general | solution.py:71
  12.0 0.7 reshape.66
  12.8 3.3 %convolution_convert_fusion.3 = bf16[24,8,512]{2,1,0:T(8,128)(2,1)S(1)} fusion(bf16[192,4096]{1,0:T(8,128)(2,1)S(1)} %copy-done.1, bf16[4096,512]{1,0:T(8,128)(2,1)} %param.15, bf16[24,8,8]{1,0,2:T(8,128)(2,1)} %reshape.66), kind=kOutput, calls=%fused_computation.6 | convolution fusion | flops 807075840 | bytes 5966848 | tf_op jit(solution)/shard_map/esr,esd->erd/dot_general | solution.py:77
  16.2 0.2 convolution_convert_fusion
  16.4 0.7 reshape.72
  17.1 6.3 %all-to-all-start = ((bf16[4,2,8192]{2,1,0:T(2,128)(2,1)}), bf16[4,2,8192]{2,1,0:T(2,128)(2,1)S(1)}, u32[]{:S(2)}, u32[]{:S(2)}) async-start(bf16[4,2,8192]{2,1,0:T(2,128)(2,1)} %reshape.72), calls=%async_computation | async-start | bytes 262144 | tf_op jit(solution)/shard_map/all_to_all | solution.py:105
  23.5 0.7 convert_reduce_fusion
  24.2 2.6 %multiply_reduce_fusion = f32[192]{0:T(256)S(1)} fusion(bf16[1,192,8192]{2,1,0:T(8,128)(2,1)} %param.17), kind=kLoop, calls=%fused_computation.1 | loop fusion | flops 4718400 | bytes 3146496 | tf_op jit(solution)/shard_map/reduce_sum | solution.py:22
  26.9 33.1 %psum.7 = f32[32]{0:T(128)S(1)} all-reduce(f32[32]{0:T(128)S(1)} %convert_reduce_fusion), channel_id=1, replica_groups=mesh['groups'=2,'dp'=4,'tgt'=4] {'dp','tgt'}, use_global_device_ids=true, to_apply=%region_8.9 | all-reduce | flops 32 | bytes 256 | tf_op jit(solution)/shard_map/psum | solution.py:60
  60.0 0.2 select_reduce_fusion
  60.2 0.6 reduce_sum.78
  60.8 0.6 dynamic-slice
  62.1 6.5 %all_gather.3 = bf16[32,8192]{1,0:T(8,128)(2,1)S(1)} all-gather(bf16[8,8192]{1,0:T(8,128)(2,1)S(1)} %reshape.73), channel_id=1, replica_groups=mesh['groups'=2,'dp'=4,'tgt'=4] {'tgt'}, dimensions={0}, use_global_device_ids=true | all-gather | bytes 655360 | tf_op jit(solution)/shard_map/all_gather | solution.py:112
  68.6 0.2 multiply_reduce_fusion.1
  68.8 3.0 %fusion.10 = f32[32,192]{1,0:T(8,128)S(1)} fusion(bf16[32,8192]{1,0:T(8,128)(2,1)S(1)} %all_gather.3, bf16[1,192,8192]{2,1,0:T(8,128)(2,1)} %param.17, f32[192]{0:T(256)S(1)} %add_rsqrt_fusion, f32[32]{0:T(128)S(1)} %rsqrt_multiply_fusion), kind=kOutput, calls=%fused_computation.14 | convolution fusion | flops 100681728 | bytes 3695488 | tf_op jit(solution)/shard_map/dot_general | solution.py:15
  71.8 0.2 fusion.20
  72.0 11.1 %all-reduce = f32[32,16]{1,0:T(8,128)S(1)} all-reduce(f32[32,16]{1,0:T(8,128)S(1)} %fusion.20), channel_id=2, replica_groups=mesh['groups'=2,'dp'=4,'tgt'=4] {'tgt'}, use_global_device_ids=true, to_apply=%region_4.5.clone | all-reduce | flops 512 | bytes 4096
  83.2 0.1 fusion.27
  83.4 7.9 %all_to_all.14 = f32[4,1,2]{2,1,0:T(1,128)S(1)} all-to-all(f32[4,1,2]{2,1,0:T(1,128)S(1)} %bitcast.45), channel_id=1, replica_groups=mesh['groups'=2,'dp'=4,'tgt'=4] {'dp'}, dimensions={0} | all-to-all | bytes 64 | tf_op jit(solution)/shard_map/all_to_all | solution.py:116
  91.3 0.5 broadcast.76
  91.8 0.7 reduce.3
  92.6 0.1 select_reduce_fusion.2
  92.6 1.1 %multiply_select_fusion = f32[24]{0:T(128)} fusion(pred[24]{0:T(512)(128)(4,1)S(1)} %compare_and_fusion, f32[24]{0:T(128)S(1)} %select_reduce_fusion.2, f32[24]{0:T(128)S(1)} %select_reduce_fusion, f32[]{:T(128)} %reduce_sum.78), kind=kLoop, calls=%fused_computation.48 | loop fusion | flops 120 | bytes 316 | tf_op jit(solution)/shard_map/jit(_where)/select_n | solution.py:122
  (19 shorter events, 0.4 us)
Async XLA Ops:
  0.0 5.6 %copy-start = (bf16[192,4096]{1,0:T(8,128)(2,1)S(1)}, bf16[192,4096]{1,0:T(8,128)(2,1)}, u32[]{:S(2)}) copy-start(bf16[192,4096]{1,0:T(8,128)(2,1)} %param.11) | copy-start | bytes 4718596
  8.9 1.2 %copy-start.2 = (bf16[64,8]{0,1:T(8,128)(2,1)S(1)}, bf16[64,8]{0,1:T(8,128)(2,1)}, u32[]{:S(2)}) copy-start(bf16[64,8]{0,1:T(8,128)(2,1)} %param.16) | copy-start | bytes 3076
  10.1 2.7 %copy-start.1 = (bf16[192,4096]{1,0:T(8,128)(2,1)S(1)}, bf16[192,4096]{1,0:T(8,128)(2,1)}, u32[]{:S(2)}) copy-start(bf16[192,4096]{1,0:T(8,128)(2,1)} %param.12) | copy-start | bytes 4718596
  17.1 44.9 %all-to-all-start = ((bf16[4,2,8192]{2,1,0:T(2,128)(2,1)}), bf16[4,2,8192]{2,1,0:T(2,128)(2,1)S(1)}, u32[]{:S(2)}, u32[]{:S(2)}) async-start(bf16[4,2,8192]{2,1,0:T(2,128)(2,1)} %reshape.72), calls=%async_computation | async-start | bytes 262144 | tf_op jit(solution)/shard_map/all_to_all | solution.py:105
  24.2 35.8 %copy-start.3 = (s32[24]{0:T(128)S(1)}, s32[24]{0:T(128)}, u32[]{:S(2)}) copy-start(s32[24]{0:T(128)} %param.18) | copy-start | bytes 292
  24.2 36.5 %copy-start.4 = (u32[32]{0:T(128)S(1)}, u32[32]{0:T(128)}, u32[]{:S(2)}) copy-start(u32[32]{0:T(128)} %constant.44) | copy-start | bytes 388
where the time goes:
time: 94.3 us; the launch traced here: 93.7 us
  blocking collectives  58.7 us (62%)
  matrix products  14.3 us (15%)
  other arithmetic  8.73 us (9%)
  starting transfers between devices  6.34 us (7%)
  local copies, waits for them, and re-layouts  4.17 us (4%)
  between operations  1.57 us (2%)
    psum x1, blocking collectives, shards(): counts = lax.psum(local_counts, ('dp', 'tgt'))  33.1 us
    unnamed x1, blocking collectives  11.1 us
    all_to_all x1, blocking collectives, shards(): lax.all_to_all(raw_owner.reshape(owner_count, CAP), 'dp', split_axis=0, c...  7.9 us
    all_gather x1, blocking collectives, shards(): row_piece = lax.all_gather(owner_rows, 'tgt', axis=0, tiled=True)  6.5 us
    all_to_all x1, starting transfers between devices, shards(): lax.all_to_all(outgoing.reshape(owner_count, CAP, -1), 'dp', split_axis=0...  6.34 us
    dot_general x1, matrix products, shards(): jnp.einsum('esr,esd->erd', per_example(rank_down, examples), per_example(...  3.33 us
    dot_general x1, matrix products, shards(): jnp.einsum('esd,esr->edr', per_example(wide_hidden, examples), per_exampl...  3.31 us
    dot_general x1, matrix products, contracted_row_sums(): lax.dot_general(row_block, col_block, (((1,), (1,)), ((), ())), preferred...  2.97 us
  transfers between devices with their start and end apart: 1, of which 0 were waited for; matrix products, arithmetic and copies ran while one was open for 5% of the time, Pallas kernels for 0%

commit v1 on v0

--- a/solution.py
+++ b/solution.py
@@ -109,7 +109,12 @@
     own_targets = targets[0]
     target_inv = inverse_norms(own_targets)
     offset = lax.axis_index("tgt") * own_targets.shape[0]
-    row_piece = lax.all_gather(owner_rows, "tgt", axis=0, tiled=True)
+    ring = [owner_rows]
+    for hop in range(3):
+        ring.append(lax.ppermute(ring[-1], "tgt", [(dev, (dev + 1) % 4) for dev in range(4)]))
+    row_piece = jnp.roll(
+        jnp.concatenate(ring[::-1], axis=0), (lax.axis_index("tgt") + 1) * ring[0].shape[0], axis=0
+    )
     partials = task_terms(row_piece, inverse_norms(row_piece), own_targets, target_inv, offset)
     task_sums = lax.psum_scatter(partials, "tgt", scatter_dimension=0, tiled=True)
     raw_owner = jnp.max(task_sums / (TGT // TASKS), axis=1)

time: 94.3 us -> 96.8 us (1.027)
  starting transfers between devices: 6.34 us -> 0.06 us
  waiting for transfers between devices: 0.01 us -> 6.06 us
  blocking collectives: 58.7 us -> 62.4 us
    all_to_all x0 -> x1, blocking collectives: none -> 12.2 us  [shards(): lax.all_to_all(outgoing.reshape(owner_count, CAP, -1), 'dp', split_axis=0...]
    all_gather x1 -> x0, blocking collectives: 6.5 us -> none  [shards(): row_piece = lax.all_gather(owner_rows, 'tgt', axis=0, tiled=True)]
    all_to_all x1 -> x0, starting transfers between devices: 6.34 us -> none  [shards(): lax.all_to_all(outgoing.reshape(owner_count, CAP, -1), 'dp', split_axis=0...]
    ppermute x0 -> x3, waiting for transfers between devices: none -> 6.06 us  [shards(): lax.ppermute(ring[-1], 'tgt', [(dev, (dev + 1) % 4) for dev in range(4)])]
    unnamed x1, blocking collectives: 11.1 us -> 10.1 us
    psum x1, blocking collectives: 33.1 us -> 32.1 us  [shards(): counts = lax.psum(local_counts, ('dp', 'tgt'))]
  transfers between devices with their start and end apart: 1 -> 3, of which waited for: 0 -> 2; matrix products, arithmetic and copies ran while one was open for 5% -> 4% of each run, Pallas kernels for 0% -> 0%
where the time goes in v1:
time: 96.8 us; the launch traced here: 96.3 us
  blocking collectives  62.4 us (64%)
  matrix products  14.2 us (15%)
  other arithmetic  8.29 us (9%)
  waiting for transfers between devices  6.06 us (6%)
  local copies, waits for them, and re-layouts  3.62 us (4%)
  between operations  1.67 us (2%)
    psum x1, blocking collectives, shards(): counts = lax.psum(local_counts, ('dp', 'tgt'))  32.1 us
    all_to_all x1, blocking collectives, shards(): lax.all_to_all(outgoing.reshape(owner_count, CAP, -1), 'dp', split_axis=0...  12.2 us
    unnamed x1, blocking collectives  10.1 us
    all_to_all x1, blocking collectives, shards(): lax.all_to_all(raw_owner.reshape(owner_count, CAP), 'dp', split_axis=0, c...  7.9 us
    ppermute x3, waiting for transfers between devices, shards(): lax.ppermute(ring[-1], 'tgt', [(dev, (dev + 1) % 4) for dev in range(4)])  6.06 us
    dot_general x1, matrix products, shards(): jnp.einsum('esr,esd->erd', per_example(rank_down, examples), per_example(...  3.33 us
    dot_general x1, matrix products, shards(): jnp.einsum('esd,esr->edr', per_example(wide_hidden, examples), per_exampl...  3.31 us
    dot_general x1, matrix products, contracted_row_sums(): lax.dot_general(row_block, col_block, (((1,), (1,)), ((), ())), preferred...  2.97 us
  transfers between devices with their start and end apart: 3, of which 2 were waited for; matrix products, arithmetic and copies ran while one was open for 4% of the time, Pallas kernels for 0%

profile of v1, /device:TPU:0, one launch (start us, length us, event | category | flops | bytes accessed | tf_op | source)
XLA Modules:
  0.0 96.3 jit_solution(10175566040631744503)
XLA Ops:
  0.8 0.7 compare_and_fusion.1
  1.4 0.9 select_reduce_fusion.1
  2.3 0.2 convert_reduce_fusion.1
  2.5 0.7 compare_and_fusion
  3.2 2.3 %fusion.15 = bf16[192,8]{0,1:T(8,128)(2,1)S(1)} fusion(bf16[64,8]{0,1:T(8,128)(2,1)} %param.16, bf16[192,4096]{1,0:T(8,128)(2,1)} %param.12, bf16[64,4096]{1,0:T(8,128)(2,1)} %param.14), kind=kOutput, calls=%fused_computation.17 | convolution fusion | flops 100873728 | bytes 2101248 | tf_op jit(solution)/shard_map/dot_general | solution.py:74
  5.5 0.1 reshape.70
  5.6 3.3 %convolution_convert_fusion.1 = bf16[24,512,8]{1,2,0:T(8,128)(2,1)S(1)} fusion(bf16[192,4096]{1,0:T(8,128)(2,1)S(1)} %copy-done, bf16[4096,512]{1,0:T(8,128)(2,1)} %param.15, bf16[24,8,8]{1,0,2:T(8,128)(2,1)S(1)} %reshape.70), kind=kOutput, calls=%fused_computation.4 | convolution fusion | flops 807075840 | bytes 5966848 | tf_op jit(solution)/shard_map/esd,esr->edr/dot_general | solution.py:83
  8.9 0.8 copy.25
  9.8 0.3 copy.26
  10.1 1.9 %fusion.16 = bf16[192,8]{0,1:T(8,128)(2,1)S(1)} fusion(bf16[64,8]{0,1:T(8,128)(2,1)S(1)} %copy-done.2, bf16[192,4096]{1,0:T(8,128)(2,1)S(1)} %copy-done, bf16[4096,64]{0,1:T(8,128)(2,1)} %param.13), kind=kOutput, calls=%fused_computation.18 | convolution fusion | flops 100873728 | bytes 2101248 | tf_op jit(solution)/shard_map/dot_general | solution.py:71
  12.0 0.7 reshape.66
  12.8 3.3 %convolution_convert_fusion.3 = bf16[24,8,512]{2,1,0:T(8,128)(2,1)S(1)} fusion(bf16[192,4096]{1,0:T(8,128)(2,1)S(1)} %copy-done.1, bf16[4096,512]{1,0:T(8,128)(2,1)} %param.15, bf16[24,8,8]{1,0,2:T(8,128)(2,1)} %reshape.66), kind=kOutput, calls=%fused_computation.6 | convolution fusion | flops 807075840 | bytes 5966848 | tf_op jit(solution)/shard_map/esr,esd->erd/dot_general | solution.py:77
  16.2 0.2 convolution_convert_fusion
  16.4 0.1 reshape.72
  16.5 12.2 %all_to_all.14 = bf16[4,2,8192]{2,1,0:T(2,128)(2,1)S(1)} all-to-all(bf16[4,2,8192]{2,1,0:T(2,128)(2,1)S(1)} %reshape.72), channel_id=1, replica_groups=mesh['groups'=2,'dp'=4,'tgt'=4] {'dp'}, dimensions={0} | all-to-all | bytes 262144 | tf_op jit(solution)/shard_map/all_to_all | solution.py:105
  28.9 2.6 %multiply_reduce_fusion = f32[192]{0:T(256)S(1)} fusion(bf16[1,192,8192]{2,1,0:T(8,128)(2,1)} %param.17), kind=kLoop, calls=%fused_computation.1 | loop fusion | flops 4718400 | bytes 3146496 | tf_op jit(solution)/shard_map/reduce_sum | solution.py:22
  31.5 1.8 %collective-permute-done = bf16[8,8192]{1,0:T(8,128)(2,1)S(1)} collective-permute-done((bf16[8,8192]{1,0:T(8,128)(2,1)S(1)}, bf16[8,8192]{1,0:T(8,128)(2,1)S(1)}, u32[]{:S(2)}, u32[]{:S(2)}) %collective-permute-start) | collective-permute-done | bytes 131104 | tf_op jit(solution)/shard_map/ppermute | solution.py:114
  33.2 0.1 convert_reduce_fusion
  33.3 4.3 %collective-permute-done.1 = bf16[8,8192]{1,0:T(8,128)(2,1)S(1)} collective-permute-done((bf16[8,8192]{1,0:T(8,128)(2,1)S(1)}, bf16[8,8192]{1,0:T(8,128)(2,1)S(1)}, u32[]{:S(2)}, u32[]{:S(2)}) %collective-permute-start.1) | collective-permute-done | bytes 131104 | tf_op jit(solution)/shard_map/ppermute | solution.py:114
  37.7 0.6 dynamic-slice
  38.9 32.1 %psum.7 = f32[32]{0:T(128)S(1)} all-reduce(f32[32]{0:T(128)S(1)} %convert_reduce_fusion), channel_id=1, replica_groups=mesh['groups'=2,'dp'=4,'tgt'=4] {'dp','tgt'}, use_global_device_ids=true, to_apply=%region_8.9 | all-reduce | flops 32 | bytes 256 | tf_op jit(solution)/shard_map/psum | solution.py:60
  71.0 0.7 reduce_sum.78
  71.7 0.2 select_reduce_fusion
  72.0 0.2 multiply_reduce_fusion.1
  72.3 3.0 %fusion.10 = f32[32,192]{1,0:T(8,128)S(1)} fusion(bf16[1,192,8192]{2,1,0:T(8,128)(2,1)} %param.17, bf16[64,8192]{1,0:T(8,128)(2,1)S(1)} %constant_dynamic-update-slice_fusion, s32[]{:T(128)S(6)} %select_n.40, f32[192]{0:T(256)S(1)} %add_rsqrt_fusion, f32[32]{0:T(128)S(1)} %rsqrt_multiply_fusion), kind=kOutput, calls=%fused_computation.14 | convolution fusion | flops 100681728 | bytes 3696132 | tf_op jit(solution)/shard_map/dot_general | solution.py:15
  75.3 0.2 fusion.21
  75.5 10.1 %all-reduce = f32[32,16]{1,0:T(8,128)S(1)} all-reduce(f32[32,16]{1,0:T(8,128)S(1)} %fusion.21), channel_id=2, replica_groups=mesh['groups'=2,'dp'=4,'tgt'=4] {'tgt'}, use_global_device_ids=true, to_apply=%region_4.5.clone | all-reduce | flops 512 | bytes 4096
  85.6 0.1 fusion.28
  85.8 7.9 %all_to_all.15 = f32[4,1,2]{2,1,0:T(1,128)S(1)} all-to-all(f32[4,1,2]{2,1,0:T(1,128)S(1)} %bitcast.44), channel_id=1, replica_groups=mesh['groups'=2,'dp'=4,'tgt'=4] {'dp'}, dimensions={0} | all-to-all | bytes 64 | tf_op jit(solution)/shard_map/all_to_all | solution.py:121
  93.7 0.5 broadcast.77
  94.3 0.7 reduce.3
  95.1 1.2 %multiply_select_fusion = f32[24]{0:T(128)} fusion(pred[24]{0:T(512)(128)(4,1)S(1)} %compare_and_fusion, f32[24]{0:T(128)S(1)} %select_reduce_fusion.2, f32[24]{0:T(128)S(1)} %select_reduce_fusion, f32[]{:T(128)} %reduce_sum.78), kind=kLoop, calls=%fused_computation.57 | loop fusion | flops 120 | bytes 316 | tf_op jit(solution)/shard_map/jit(_where)/select_n | solution.py:127
  (31 shorter events, 0.6 us)
Async XLA Ops:
  0.0 5.6 %copy-start = (bf16[192,4096]{1,0:T(8,128)(2,1)S(1)}, bf16[192,4096]{1,0:T(8,128)(2,1)}, u32[]{:S(2)}) copy-start(bf16[192,4096]{1,0:T(8,128)(2,1)} %param.11) | copy-start | bytes 4718596
  8.9 1.2 %copy-start.2 = (bf16[64,8]{0,1:T(8,128)(2,1)S(1)}, bf16[64,8]{0,1:T(8,128)(2,1)}, u32[]{:S(2)}) copy-start(bf16[64,8]{0,1:T(8,128)(2,1)} %param.16) | copy-start | bytes 3076
  10.1 2.7 %copy-start.1 = (bf16[192,4096]{1,0:T(8,128)(2,1)S(1)}, bf16[192,4096]{1,0:T(8,128)(2,1)}, u32[]{:S(2)}) copy-start(bf16[192,4096]{1,0:T(8,128)(2,1)} %param.12) | copy-start | bytes 4718596
  28.8 4.5 %copy-start.3 = (s32[24]{0:T(128)S(1)}, s32[24]{0:T(128)}, u32[]{:S(2)}) copy-start(s32[24]{0:T(128)} %param.18) | copy-start | bytes 292
  28.8 8.9 %copy-start.4 = (u32[32]{0:T(128)S(1)}, u32[32]{0:T(128)}, u32[]{:S(2)}) copy-start(u32[32]{0:T(128)} %constant.68) | copy-start | bytes 388
  28.8 4.4 %collective-permute-start = (bf16[8,8192]{1,0:T(8,128)(2,1)S(1)}, bf16[8,8192]{1,0:T(8,128)(2,1)S(1)}, u32[]{:S(2)}, u32[]{:S(2)}) collective-permute-start(bf16[8,8192]{1,0:T(8,128)(2,1)S(1)} %reshape.73), channel_id=1, source_target_pairs={{0,1},{1,2},{2,3},{3,0},{4,5},{5,6},{6,7},{7,4},{8,9},{9,10},{10,1... | collective-permute-start | bytes 393224 | tf_op jit(solution)/shard_map/ppermute | solution.py:114
  33.2 4.4 %collective-permute-start.1 = (bf16[8,8192]{1,0:T(8,128)(2,1)S(1)}, bf16[8,8192]{1,0:T(8,128)(2,1)S(1)}, u32[]{:S(2)}, u32[]{:S(2)}) collective-permute-start(bf16[8,8192]{1,0:T(8,128)(2,1)S(1)} %collective-permute-done), channel_id=1, source_target_pairs={{0,1},{1,2},{2,3},{3,0},{4,5},{5,6},{6,7},{7,4},{8,9},{9,10},{10,1... | collective-permute-start | bytes 393224 | tf_op jit(solution)/shard_map/ppermute | solution.py:114
  37.6 34.3 %collective-permute-start.2 = (bf16[8,8192]{1,0:T(8,128)(2,1)S(1)}, bf16[8,8192]{1,0:T(8,128)(2,1)S(1)}, u32[]{:S(2)}, u32[]{:S(2)}) collective-permute-start(bf16[8,8192]{1,0:T(8,128)(2,1)S(1)} %collective-permute-done.1), channel_id=1, source_target_pairs={{0,1},{1,2},{2,3},{3,0},{4,5},{5,6},{6,7},{7,4},{8,9},{9,10},{10,1... | collective-permute-start | bytes 393224 | tf_op jit(solution)/shard_map/ppermute | solution.py:114
